TPU v7x, 256 devices: a whole 4x4x8 slice. The times are simulated.
256 devices in a mesh: row: 32 (over x, y, core), col: 8 (over z).
Axes of the slice: x: 4, y: 4, z: 8, core: 2. Of those that a mesh axis runs over, the one named last changes fastest.
Arguments:
- tile_values: bfloat16 [24576, 256, 256], P(('row', 'col')), may hold values from -0.375 to 0.375
- tile_coords: int32 [24576, 2], P(('row', 'col')), may hold values from 0 to 15, as said below
- live_counts: int32 [256], P(('row', 'col')), may hold values from 24 to 96, as said below
Outputs:
- range_basis: float32 [131072, 192], P(('row', 'col'))
- projected: float32 [8, 4096, 192], P('col', 'row')
Inputs may be any that keep to these rules, and one draw needn't show every extreme that they name: `tile_coords`: for each device, column 0 is below 16, column 1 is below 16, and the 96 positions of its slots are distinct. `live_counts`: some device has all 96 slots live.
All inputs are finite; a program needn't handle non-finite values.
Results may differ from a plain program's by a relative error of at most 0.0003.
Values sent between devices are 32-bit elements; how exact they have to be, the bound alone decides.
No kernel may reach another device: no remote copies, remote signals or barrier semaphores. Data moves between devices by JAX's collectives and lax.ppermute only.
A program may use at most 128 MiB of HBM per device.

v0:
```python
import math
import jax
import jax.numpy as jnp
from jax import lax
from jax.sharding import PartitionSpec as P

TB = 256
K = 192
RT = 16
CT = 16


def sketch_signs(column_ids, rank_cols):
    rank_index = jnp.arange(rank_cols, dtype=jnp.int32)
    hashed = column_ids[..., None] * rank_cols + rank_index
    hashed = hashed * 747796405 + 1442695040
    hashed = hashed ^ hashed >> 15
    hashed = hashed * 1103515245 + 12345
    hashed = hashed ^ hashed >> 13
    return (1 - 2 * (hashed >> 9 & 1)).astype(jnp.float32)


def basis_from(sketch_rows, gram_matrix, basis_scale):
    factor = jnp.linalg.cholesky(gram_matrix)
    solved = jax.scipy.linalg.solve_triangular(factor, sketch_rows.T, lower=True)
    return basis_scale * solved.T


def per_device(tile_values, tile_coords, live_counts):
    slot_count = tile_values.shape[0]
    col_index = lax.axis_index("col")
    tile_row = tile_coords[:, 0]
    tile_col = tile_coords[:, 1]
    live_mask = (jnp.arange(slot_count, dtype=jnp.int32) < live_counts[0]).astype(jnp.float32)[
        :, None, None
    ]
    column_ids = (
        col_index * (CT * TB) + tile_col[:, None] * TB + jnp.arange(TB, dtype=jnp.int32)[None, :]
    )
    test_signs = sketch_signs(column_ids, K).astype(jnp.bfloat16)
    sketch_terms = (
        jnp.einsum("tij,tjk->tik", tile_values, test_signs, preferred_element_type=jnp.float32)
        * live_mask
    )
    sketch_part = jax.ops.segment_sum(sketch_terms, tile_row, num_segments=RT).reshape(RT * TB, K)
    basis_scale = math.sqrt(RT * TB * lax.axis_size("row"))
    sketch_full = lax.psum(sketch_part, "col")
    gram_local = jnp.dot(
        sketch_full.T,
        sketch_full,
        precision=lax.Precision.HIGHEST,
        preferred_element_type=jnp.float32,
    )
    gram_matrix = lax.psum(gram_local, "row")
    basis_full = basis_from(sketch_full, gram_matrix, basis_scale)
    share_rows = RT * TB // lax.axis_size("col")
    range_basis = lax.dynamic_slice_in_dim(basis_full, col_index * share_rows, share_rows, 0)
    picked = basis_full.reshape(RT, TB, K)[tile_row]
    adjoint_terms = (
        jnp.einsum(
            "tij,tik->tjk",
            tile_values,
            picked,
            precision=lax.Precision.HIGHEST,
            preferred_element_type=jnp.float32,
        )
        * live_mask
    )
    adjoint_part = jax.ops.segment_sum(adjoint_terms, tile_col, num_segments=CT).reshape(CT * TB, K)
    projected = lax.psum_scatter(adjoint_part, "row", scatter_dimension=0, tiled=True)
    return (range_basis, projected[None])


def solution(mesh):
    in_specs = (P(("row", "col"), None, None), P(("row", "col"), None), P(("row", "col")))
    out_specs = (P(("row", "col"), None), P("col", "row", None))
    return jax.shard_map(
        per_device, mesh=mesh, in_specs=in_specs, out_specs=out_specs, check_vma=False
    )
```

profile of v0, /device:TPU:2, one launch (start us, length us, event | category | flops | bytes accessed | tf_op | source)
XLA Modules:
  0.0 484.5 jit_solution(14673898791970698551)
XLA Ops:
  7.2 0.8 fusion.31
  8.7 16.9 %multiply_bitcast_fusion.1 = f32[96,256,192]{1,2,0:T(8,128)} fusion(f32[96]{0:T(128)S(1)} %compare_convert_fusion, bf16[96,256,256]{2,1,0:T(8,128)(2,1)} %param.3, s32[96,256]{1,0:T(8,128)S(1)} %add_multiply_fusion), kind=kOutput, calls=%fused_computation.14 | convolution fusion | flops 2491416576 | bytes 31555968 | tf_op jit(solution)/shard_map/tij,tjk->tik/dot_general | solution.py:42
  25.9 29.1 %scatter_fusion = f32[16,256,192]{1,2,0:T(8,128)S(1)} fusion(f32[16,256,192]{1,2,0:T(8,128)S(1)} %broadcast.151.clone, s32[96]{0:T(128)S(1)} %get-tuple-element.29, f32[96,256,192]{1,2,0:T(8,128)} %multiply_bitcast_fusion.1), kind=kCustom, calls=%fused_computation.1 | custom fusion | flops 4718592 | bytes 56623488 | tf_op jit(solution)/shard_map/scatter-add | solution.py:45
  55.1 2.1 copy.14
  57.3 94.5 %all-reduce.6.cloned.1.call-done = f32[4096,192]{0,1:T(8,128)} async-done(((f32[4096,192]{0,1:T(8,128)}), f32[4096,192]{0,1:T(8,128)}) %all-reduce.6.cloned.1.call-update) | async-done | bytes 3145744 | tf_op jit(solution)/shard_map/psum | solution.py:47
  151.7 6.2 %fusion.41 = f32[192,192]{0,1:T(8,128)} fusion(f32[4096,192]{0,1:T(8,128)} %all-reduce.6.cloned.1.call-done), kind=kOutput, calls=%fused_computation.78 | convolution fusion | flops 1811939328 | bytes 3293184 | tf_op jit(solution)/shard_map/dot_general | solution.py:48
  158.2 109.3 %all-reduce.8.cloned.1.call-done = f32[192,192]{0,1:T(8,128)} async-done(((f32[192,192]{0,1:T(8,128)}), f32[192,192]{0,1:T(8,128)}) %all-reduce.8.cloned.1.call-update) | async-done | bytes 147472 | tf_op jit(solution)/shard_map/psum | solution.py:54
  267.5 1.0 copy.9
  268.6 1.0 fusion.24
  269.5 11.7 %cholesky.51 = f32[128,128]{1,0:T(8,128)S(1)} custom-call(f32[128,128]{1,0:T(8,128)S(1)} %cholesky.124), custom_call_target="Cholesky" | custom-call | tf_op jit(solution)/shard_map/jit(cholesky)/cholesky | solution.py:24
  281.3 9.8 %custom-call.15 = f32[1,128,128]{1,2,0:T(8,128)S(1)} custom-call(f32[1,128,128]{2,1,0:T(8,128)S(1)} %get-tuple-element.23), custom_call_target="InvertDiagBlocksLowerTriangular" | custom-call | tf_op jit(solution)/shard_map/jit(cholesky)/cholesky | solution.py:24
  291.5 5.8 %cholesky.110 = f32[64,64]{1,0:T(8,128)S(1)} custom-call(f32[64,64]{1,0:T(8,128)S(1)} %convolution_subtract_fusion.1), custom_call_target="Cholesky" | custom-call | tf_op jit(solution)/shard_map/jit(cholesky)/cholesky | solution.py:24
  297.4 0.6 compare_reduce_fusion
  300.1 19.9 %custom-call.16 = f32[2,128,128]{1,2,0:T(8,128)S(1)} custom-call(f32[2,128,128]{2,1,0:T(8,128)S(1)} %pad_maximum_fusion), custom_call_target="InvertDiagBlocksLowerTriangular" | custom-call | tf_op jit(solution)/shard_map/jit(_solve_triangular)/triangular_solve | solution.py:25
  320.0 3.5 fusion.22
  323.5 2.4 convolution_subtract_fusion
  326.0 1.0 fusion.29
  327.4 1.6 copy-done
  329.4 8.2 %gather_fusion = f32[96,256,192]{1,2,0:T(8,128)} fusion(f32[16,256,192]{1,2,0:T(8,128)S(1)} %bitcast.57, s32[1024]{0:T(1024)S(1)} %pad_clamp_fusion), kind=kCustom, calls=%fused_computation | custom fusion | bytes 37749120 | tf_op jit(solution)/shard_map/gather | solution.py:58
  337.6 21.8 %multiply_bitcast_fusion = f32[96,256,192]{1,2,0:T(8,128)} fusion(f32[96]{0:T(128)S(1)} %compare_convert_fusion, f32[96,256,192]{1,2,0:T(8,128)} %gather_fusion, bf16[96,256,256]{2,1,0:T(8,128)(2,1)} %param.3), kind=kOutput, calls=%fused_computation.13 | convolution fusion | flops 14500233216 | bytes 50332032 | tf_op jit(solution)/shard_map/tij,tik->tjk/dot_general | solution.py:60
  359.7 29.1 %scatter_fusion.1 = f32[16,256,192]{1,2,0:T(8,128)S(1)} fusion(f32[16,256,192]{1,2,0:T(8,128)S(1)} %broadcast.151, s32[96]{0:T(128)S(1)} %get-tuple-element.27, f32[96,256,192]{1,2,0:T(8,128)} %multiply_bitcast_fusion), kind=kCustom, calls=%fused_computation.2 | custom fusion | flops 4718592 | bytes 56623488 | tf_op jit(solution)/shard_map/scatter-add | solution.py:69
  388.8 2.1 copy.15
  390.9 1.8 dynamic-slice_bitcast_fusion
  392.7 85.3 %reduce-scatter.2.cloned.1.call-done = f32[128,192]{0,1:T(8,128)} async-done(((f32[4096,192]{0,1:T(8,128)}), f32[128,192]{0,1:T(8,128)}) %reduce-scatter.2.cloned.1.call-update) | async-done | bytes 98320 | tf_op jit(solution)/shard_map/reduce_scatter | solution.py:70
  (27 shorter events, 3.0 us)
Async XLA Ops:
  7.2 144.6 %all-reduce.6.cloned.1.call-start = ((), (), s32[]{:S(2)}) async-start(), calls=%async_computation.1 | async-start | bytes 6291456 | tf_op jit(solution)/shard_map/psum | solution.py:47
  57.2 210.3 %all-reduce.8.cloned.1.call-start = ((), (), s32[]{:S(2)}) async-start(), calls=%async_computation.2 | async-start | bytes 393216 | tf_op jit(solution)/shard_map/psum | solution.py:54
  157.9 320.0 %reduce-scatter.2.cloned.1.call-start = ((), (), s32[]{:S(2)}) async-start(), calls=%async_computation.3 | async-start | bytes 3244032 | tf_op jit(solution)/shard_map/reduce_scatter | solution.py:70
  327.4 1.6 copy-start
Sparse Core Ops, SparseCore 0:
  57.3 94.3 all-reduce.5
  158.1 109.3 all-reduce.7
  391.0 86.8 reduce-scatter.1
where the time goes:
time: 485 us; the launch traced here: 484 us
  waiting for transfers between devices  289 us (60%)
  other arithmetic  109 us (22%)
  matrix products  52.2 us (11%)
  local copies, waits for them, and re-layouts  17.8 us (4%)
  between operations  15.9 us (3%)
    psum x1, waiting for transfers between devices, per_device(): gram_matrix = lax.psum(gram_local, 'row')  109 us
    psum x1, waiting for transfers between devices, per_device(): sketch_full = lax.psum(sketch_part, 'col')  94.5 us
    reduce_scatter x1, waiting for transfers between devices, per_device(): lax.psum_scatter(adjoint_part, 'row', scatter_dimension=0, tiled=True)  85.3 us
    scatter-add x1, other arithmetic, per_device(): jax.ops.segment_sum(sketch_terms, tile_row, num_segments=RT)  29.1 us
    scatter-add x1, other arithmetic, per_device(): jax.ops.segment_sum(adjoint_terms, tile_col, num_segments=CT)  29.1 us
    another operation x7, other arithmetic, basis_from(): factor = jnp.linalg.cholesky(gram_matrix)  28.7 us
    dot_general x1, matrix products, per_device(): jnp.einsum('tij,tik->tjk', tile_values, picked, precision=lax.Precision.H...  21.8 us
    another operation x6, other arithmetic, basis_from(): jax.scipy.linalg.solve_triangular(factor, sketch_rows.T, lower=True)  20 us
  transfers between devices with their start and end apart: 3, of which 3 were waited for; matrix products, arithmetic and copies ran while one was open for 0% of the time, Pallas kernels for 0%

commit v1 on v0

--- a/solution.py
+++ b/solution.py
@@ -51,7 +51,8 @@
         precision=lax.Precision.HIGHEST,
         preferred_element_type=jnp.float32,
     )
-    gram_matrix = lax.psum(gram_local, "row")
+    parts = lax.all_gather(gram_local, "row")
+    gram_matrix = jnp.sum(parts, axis=0)
     basis_full = basis_from(sketch_full, gram_matrix, basis_scale)
     share_rows = RT * TB // lax.axis_size("col")
     range_basis = lax.dynamic_slice_in_dim(basis_full, col_index * share_rows, share_rows, 0)

time: 485 us -> 430 us (0.89)
  waiting for transfers between devices: 289 us -> 232 us
    psum x1 -> x0, waiting for transfers between devices: 109 us -> none  [per_device(): gram_matrix = lax.psum(gram_local, 'row')]
    all_gather x0 -> x1, waiting for transfers between devices: none -> 51.6 us  [per_device(): parts = lax.all_gather(gram_local, 'row')]
where the time goes in v1:
time: 430 us; the launch traced here: 429 us
  waiting for transfers between devices  232 us (54%)
  other arithmetic  112 us (26%)
  matrix products  52.2 us (12%)
  local copies, waits for them, and re-layouts  16.8 us (4%)
  between operations  15.9 us (4%)
    psum x1, waiting for transfers between devices, per_device(): sketch_full = lax.psum(sketch_part, 'col')  94.5 us
    reduce_scatter x1, waiting for transfers between devices, per_device(): lax.psum_scatter(adjoint_part, 'row', scatter_dimension=0, tiled=True)  86 us
    all_gather x1, waiting for transfers between devices, per_device(): parts = lax.all_gather(gram_local, 'row')  51.6 us
    scatter-add x1, other arithmetic, per_device(): jax.ops.segment_sum(sketch_terms, tile_row, num_segments=RT)  29.1 us
    scatter-add x1, other arithmetic, per_device(): jax.ops.segment_sum(adjoint_terms, tile_col, num_segments=CT)  29.1 us
    another operation x7, other arithmetic, basis_from(): factor = jnp.linalg.cholesky(gram_matrix)  28.7 us
    dot_general x1, matrix products, per_device(): jnp.einsum('tij,tik->tjk', tile_values, picked, precision=lax.Precision.H...  21.8 us
    another operation x6, other arithmetic, basis_from(): jax.scipy.linalg.solve_triangular(factor, sketch_rows.T, lower=True)  20 us
  transfers between devices with their start and end apart: 3, of which 3 were waited for; matrix products, arithmetic and copies ran while one was open for 0% of the time, Pallas kernels for 0%

profile of v1, /device:TPU:2, one launch (start us, length us, event | category | flops | bytes accessed | tf_op | source)
XLA Modules:
  0.0 428.9 jit_solution(9393843015666300661)
XLA Ops:
  7.2 0.8 fusion.31
  8.7 16.9 %multiply_bitcast_fusion.1 = f32[96,256,192]{1,2,0:T(8,128)} fusion(f32[96]{0:T(128)S(1)} %compare_convert_fusion, bf16[96,256,256]{2,1,0:T(8,128)(2,1)} %param.3, s32[96,256]{1,0:T(8,128)S(1)} %add_multiply_fusion), kind=kOutput, calls=%fused_computation.14 | convolution fusion | flops 2491416576 | bytes 31555968 | tf_op jit(solution)/shard_map/tij,tjk->tik/dot_general | solution.py:42
  25.9 29.1 %scatter_fusion = f32[16,256,192]{1,2,0:T(8,128)S(1)} fusion(f32[16,256,192]{1,2,0:T(8,128)S(1)} %broadcast.151.clone, s32[96]{0:T(128)S(1)} %get-tuple-element.29, f32[96,256,192]{1,2,0:T(8,128)} %multiply_bitcast_fusion.1), kind=kCustom, calls=%fused_computation.1 | custom fusion | flops 4718592 | bytes 56623488 | tf_op jit(solution)/shard_map/scatter-add | solution.py:45
  55.1 2.1 copy.15
  57.2 94.5 %all-reduce.5.cloned.1.call-done = f32[4096,192]{0,1:T(8,128)} async-done(((f32[4096,192]{0,1:T(8,128)}), f32[4096,192]{0,1:T(8,128)}) %all-reduce.5.cloned.1.call-update) | async-done | bytes 3145744 | tf_op jit(solution)/shard_map/psum | solution.py:47
  151.7 6.2 %fusion.41 = f32[192,192]{1,0:T(8,128)} fusion(f32[4096,192]{0,1:T(8,128)} %all-reduce.5.cloned.1.call-done), kind=kOutput, calls=%fused_computation.78 | convolution fusion | flops 1811939328 | bytes 3293184 | tf_op jit(solution)/shard_map/dot_general | solution.py:48
  158.2 51.6 %all-gather.3.cloned.1.call-done = f32[6144,192]{1,0:T(8,128)} async-done(((f32[192,192]{1,0:T(8,128)}), f32[6144,192]{1,0:T(8,128)}) %all-gather.3.cloned.1.call-update) | async-done | bytes 4718608 | tf_op jit(solution)/shard_map/all_gather | solution.py:54
  209.7 3.2 reduce_sum.9
  213.2 11.7 %cholesky.51 = f32[128,128]{1,0:T(8,128)S(1)} custom-call(f32[128,128]{1,0:T(8,128)S(1)} %cholesky.124), custom_call_target="Cholesky" | custom-call | tf_op jit(solution)/shard_map/jit(cholesky)/cholesky | solution.py:24
  224.9 9.8 %custom-call.15 = f32[1,128,128]{1,2,0:T(8,128)S(1)} custom-call(f32[1,128,128]{2,1,0:T(8,128)S(1)} %get-tuple-element.23), custom_call_target="InvertDiagBlocksLowerTriangular" | custom-call | tf_op jit(solution)/shard_map/jit(cholesky)/cholesky | solution.py:24
  235.1 5.8 %cholesky.110 = f32[64,64]{1,0:T(8,128)S(1)} custom-call(f32[64,64]{1,0:T(8,128)S(1)} %convolution_subtract_fusion.1), custom_call_target="Cholesky" | custom-call | tf_op jit(solution)/shard_map/jit(cholesky)/cholesky | solution.py:24
  241.0 0.6 compare_reduce_fusion
  241.6 0.6 compare_reduce_fusion.1
  243.7 19.9 %custom-call.16 = f32[2,128,128]{1,2,0:T(8,128)S(1)} custom-call(f32[2,128,128]{2,1,0:T(8,128)S(1)} %pad_maximum_fusion), custom_call_target="InvertDiagBlocksLowerTriangular" | custom-call | tf_op jit(solution)/shard_map/jit(_solve_triangular)/triangular_solve | solution.py:25
  263.6 3.5 fusion.22
  267.1 2.4 convolution_subtract_fusion
  269.6 1.0 fusion.29
  271.0 1.6 copy-done
  273.0 8.2 %gather_fusion = f32[96,256,192]{1,2,0:T(8,128)} fusion(f32[16,256,192]{1,2,0:T(8,128)S(1)} %bitcast.58, s32[1024]{0:T(1024)S(1)} %pad_clamp_fusion), kind=kCustom, calls=%fused_computation | custom fusion | bytes 37749120 | tf_op jit(solution)/shard_map/gather | solution.py:59
  281.2 21.8 %multiply_bitcast_fusion = f32[96,256,192]{1,2,0:T(8,128)} fusion(f32[96]{0:T(128)S(1)} %compare_convert_fusion, f32[96,256,192]{1,2,0:T(8,128)} %gather_fusion, bf16[96,256,256]{2,1,0:T(8,128)(2,1)} %param.3), kind=kOutput, calls=%fused_computation.13 | convolution fusion | flops 14500233216 | bytes 50332032 | tf_op jit(solution)/shard_map/tij,tik->tjk/dot_general | solution.py:61
  303.3 29.1 %scatter_fusion.1 = f32[16,256,192]{1,2,0:T(8,128)S(1)} fusion(f32[16,256,192]{1,2,0:T(8,128)S(1)} %broadcast.151, s32[96]{0:T(128)S(1)} %get-tuple-element.27, f32[96,256,192]{1,2,0:T(8,128)} %multiply_bitcast_fusion), kind=kCustom, calls=%fused_computation.2 | custom fusion | flops 4718592 | bytes 56623488 | tf_op jit(solution)/shard_map/scatter-add | solution.py:70
  332.4 2.1 copy.16
  334.5 1.8 dynamic-slice_bitcast_fusion
  336.3 86.0 %reduce-scatter.2.cloned.1.call-done = f32[128,192]{0,1:T(8,128)} async-done(((f32[4096,192]{0,1:T(8,128)}), f32[128,192]{0,1:T(8,128)}) %reduce-scatter.2.cloned.1.call-update) | async-done | bytes 98320 | tf_op jit(solution)/shard_map/reduce_scatter | solution.py:71
  (28 shorter events, 2.5 us)
Async XLA Ops:
  7.2 144.5 %all-reduce.5.cloned.1.call-start = ((), (), s32[]{:S(2)}) async-start(), calls=%async_computation.1 | async-start | bytes 6291456 | tf_op jit(solution)/shard_map/psum | solution.py:47
  57.1 152.6 %all-gather.3.cloned.1.call-start = ((), (), s32[]{:S(2)}) async-start(), calls=%async_computation.3 | async-start | bytes 6488064 | tf_op jit(solution)/shard_map/all_gather | solution.py:54
  157.9 264.4 %reduce-scatter.2.cloned.1.call-start = ((), (), s32[]{:S(2)}) async-start(), calls=%async_computation.2 | async-start | bytes 3244032 | tf_op jit(solution)/shard_map/reduce_scatter | solution.py:71
  271.0 1.6 copy-start
Sparse Core Ops, SparseCore 0:
  57.3 94.3 all-reduce.4
  158.0 51.6 all-gather.2
  334.6 87.6 reduce-scatter.1
